TPU v7x, 32 devices: a whole 2x2x4 slice. The times are simulated.
32 devices in a mesh: layers: 2 (over x), col: 16 (over z, y, core).
Axes of the slice: x: 2, y: 2, z: 4, core: 2. Of those that a mesh axis runs over, the one named last changes fastest.
Arguments:
- dense_weight: float32 [64, 16384], P('layers', 'col'), parts along dimension 0, may hold values from -6 to 6
- start_weight: float32 [64, 16384], P('layers', 'col'), parts along dimension 0, may hold values from -6 to 6
- keep_mask: int32 [64, 16384], P('layers', 'col'), parts along dimension 0, may hold values 0 or 1
- tile_plan: int32 [1056, 2], P(('layers', 'col')), parts along dimension 0, may hold values from 0 to 31, as said below
- hess_tiles: float32 [1056, 512, 512], P(('layers', 'col')), parts along dimension 0, as said below
Outputs:
- weights_out: float32 [64, 16384], P('layers', 'col'), parts along dimension 0
- velocity_out: float32 [64, 16384], P('layers', 'col'), parts along dimension 0
There are 2 independent parts, one for each index of `layers`. A program takes and returns all parts, laid end to end along the dimension named above; each array names one. Nothing has to cross between parts.
Inputs may be any that keep to these rules, and one draw needn't show every extreme that they name: `tile_plan`: each live slot names a tile (a, b) with a >= b, and each of the 32 (33) / 2 lower-triangle tiles is named by exactly one slot; the other slots name (0, 0). `hess_tiles`: the tiles of a symmetric positive definite matrix at the places that tile_plan names; slots that name no tile hold zeros.
All inputs are finite; a program needn't handle non-finite values. No bound on the sum of `keep_mask` on one device may be relied on, other than what follows from the above.
Results may differ from a plain program's by a relative error of at most 0.0001.
Values sent between devices are 32-bit elements; how exact they have to be, the bound alone decides.
A program may use at most 64 MiB of HBM per device.

v0:
```python
import jax
import jax.numpy as jnp
from jax import lax
from jax.sharding import PartitionSpec as P

ITERS = 2


step_size = 0.15
momentum = 0.6


def add_term(acc, piece, source, target, tile, flipped, allowed):
    order = tile.shape[1]
    span = piece.shape[1]
    tile_dim = 1 if flipped else 0
    relative = source * order
    valid = allowed & (relative >= 0) & (relative < span)

    def apply_term(total):
        block = lax.dynamic_slice_in_dim(piece, jnp.clip(relative, 0, span - order), order, 1)
        contrib = lax.dot_general(
            block,
            tile,
            (((1,), (tile_dim,)), ((), ())),
            precision=lax.Precision.HIGHEST,
            preferred_element_type=jnp.float32,
        )
        current = lax.dynamic_slice_in_dim(total, target * order, order, 1)
        return lax.dynamic_update_slice_in_dim(total, current + contrib, target * order, 1)

    def keep_total(total):
        return total

    return lax.cond(valid, apply_term, keep_total, acc)


def tile_terms(carry, piece, tile_plan, hess_tiles):

    def one_slot(slot, acc):
        row_block = tile_plan[slot, 0]
        col_block = tile_plan[slot, 1]
        tile = hess_tiles[slot]
        acc = add_term(acc, piece, row_block, col_block, tile, False, jnp.bool_(True))
        acc = add_term(acc, piece, col_block, row_block, tile, True, row_block != col_block)
        return acc

    return lax.fori_loop(0, tile_plan.shape[0], one_slot, carry)


def body(dense_weight, start_weight, keep_mask, tile_plan, hess_tiles):
    keep = keep_mask.astype(jnp.float32)
    weights = start_weight
    velocity = jnp.zeros(start_weight.shape, jnp.float32)
    full_width = dense_weight.shape[1] * lax.axis_size("col")
    for step in range(ITERS):
        error = weights - dense_weight
        empty = jnp.zeros((dense_weight.shape[0], full_width), jnp.float32)
        whole = lax.all_gather(error, "col", axis=1, tiled=True)
        partial_grad = tile_terms(empty, whole, tile_plan, hess_tiles)
        gradient = lax.psum_scatter(partial_grad, "col", scatter_dimension=1, tiled=True)
        velocity = momentum * velocity + gradient
        weights = keep * (weights - step_size * velocity)
    return (weights, velocity)


def solution(mesh):
    placed = (
        P("layers", "col"),
        P("layers", "col"),
        P("layers", "col"),
        P(("layers", "col"), None),
        P(("layers", "col"), None, None),
    )
    return jax.shard_map(
        body,
        mesh=mesh,
        in_specs=placed,
        out_specs=(P("layers", "col"), P("layers", "col")),
        check_vma=False,
    )
```

profile of v0, /device:TPU:0, one launch (start us, length us, event | category | flops | bytes accessed | tf_op | source)
XLA Modules:
  0.0 842.5 jit_solution(4746795135078019642)
XLA Ops:
  8.9 46.0 %all-gather.3.cloned.1.call-done = f32[32,16384]{1,0:T(8,128)} async-done(((f32[32,1024]{1,0:T(8,128)}), f32[32,16384]{1,0:T(8,128)}) %all-gather.3.cloned.1.call-update) | async-done | bytes 2097168 | tf_op jit(solution)/shard_map/all_gather | solution.py:59
  55.1 311.2 %while.32 = (s32[]{:T(128)}, f32[32,16384]{1,0:T(8,128)S(1)}, s32[33,2]{0,1:T(2,128)S(1)}, f32[33,512,512]{2,1,0:T(8,128)}, f32[32,16384]{1,0:T(8,128)}, /*index=5*/s32[]{:T(128)}, s32[]{:T(128)}, s32[]{:T(128)}, s32[]{:T(128)}) while((s32[]{:T(128)}, f32[32,16384]{1,0:T(8,128)S(1)}, s32[33,2]{0,1:T(2,128)S(1)}, f32[33,512,512]{2,1,0:T(8,128)}, ...), condition=%wide.region_5.6_spmd, body=%wide.region_0.5_spmd.sunk | while | flops 201359392 | bytes 4587977 | solution.py:48
  61.9 2.6 conditional.9
  71.3 2.6 conditional.9
  80.8 2.6 conditional.9
  90.2 2.6 conditional.9
  99.6 2.6 conditional.9
  109.1 2.6 conditional.9
  118.5 2.6 conditional.9
  128.0 2.6 conditional.9
  137.4 2.6 conditional.9
  146.8 2.6 conditional.9
  156.2 2.6 conditional.9
  165.6 2.6 conditional.9
  175.1 2.6 conditional.9
  184.5 2.6 conditional.9
  193.9 2.6 conditional.9
  203.3 2.6 conditional.9
  212.8 2.6 conditional.9
  222.2 2.6 conditional.9
  231.7 2.6 conditional.9
  241.1 2.6 conditional.9
  250.5 2.6 conditional.9
  260.0 2.6 conditional.9
  269.4 2.6 conditional.9
  278.8 2.6 conditional.9
  288.3 2.6 conditional.9
  297.7 2.6 conditional.9
  307.1 2.6 conditional.9
  316.5 2.6 conditional.9
  326.0 2.6 conditional.9
  335.4 2.6 conditional.9
  344.9 2.6 conditional.9
  354.3 2.6 conditional.9
  363.7 2.6 conditional.9
  367.8 59.4 %reduce-scatter.3.cloned.1.call-done = f32[32,1024]{1,0:T(8,128)} async-done(((f32[32,16384]{1,0:T(8,128)}), f32[32,1024]{1,0:T(8,128)}) %reduce-scatter.3.cloned.1.call-update) | async-done | bytes 131088 | tf_op jit(solution)/shard_map/reduce_scatter | solution.py:61
  428.8 41.5 %all-gather.5.cloned.1.call-done = f32[32,16384]{1,0:T(8,128)} async-done(((f32[32,1024]{1,0:T(8,128)}), f32[32,16384]{1,0:T(8,128)}) %all-gather.5.cloned.1.call-update) | async-done | bytes 2097168 | tf_op jit(solution)/shard_map/all_gather | solution.py:59
  470.5 303.0 %while.33 = (s32[]{:T(128)}, f32[32,16384]{1,0:T(8,128)S(1)}, s32[33,2]{0,1:T(2,128)S(1)}, f32[33,512,512]{2,1,0:T(8,128)}, f32[32,16384]{1,0:T(8,128)}, /*index=5*/s32[]{:T(128)}, s32[]{:T(128)}, s32[]{:T(128)}, s32[]{:T(128)}) while((s32[]{:T(128)}, f32[32,16384]{1,0:T(8,128)S(1)}, s32[33,2]{0,1:T(2,128)S(1)}, f32[33,512,512]{2,1,0:T(8,128)}, ...), condition=%wide.region_12.13_spmd, body=%wide.region_7.12_spmd.sunk | while | flops 201359392 | bytes 4587977 | solution.py:48
  477.1 2.5 conditional.11
  486.3 2.5 conditional.11
  495.5 2.5 conditional.11
  504.7 2.5 conditional.11
  513.9 2.5 conditional.11
  523.1 2.5 conditional.11
  532.3 2.5 conditional.11
  541.4 2.5 conditional.11
  550.6 2.5 conditional.11
  569.0 2.5 conditional.11
  578.1 2.5 conditional.11
  596.4 2.5 conditional.11
  614.8 2.5 conditional.11
  624.0 2.5 conditional.11
  642.4 2.5 conditional.11
  651.6 2.5 conditional.11
  670.0 2.5 conditional.11
  679.1 2.5 conditional.11
  697.5 2.5 conditional.11
  706.7 2.5 conditional.11
  715.8 2.5 conditional.11
  734.2 2.5 conditional.11
  743.4 2.5 conditional.11
  761.8 2.5 conditional.11
  771.0 2.5 conditional.11
  774.9 59.4 %reduce-scatter.5.cloned.1.call-done = f32[32,1024]{1,0:T(8,128)} async-done(((f32[32,16384]{1,0:T(8,128)}), f32[32,1024]{1,0:T(8,128)}) %reduce-scatter.5.cloned.1.call-update) | async-done | bytes 131088 | tf_op jit(solution)/shard_map/reduce_scatter | solution.py:61
  (365 shorter events, 539.1 us)
Async XLA Ops:
  7.2 48.0 %copy-start.6 = (s32[33,2]{0,1:T(2,128)S(1)}, s32[33,2]{0,1:T(2,128)}, u32[]{:S(2)}) copy-start(s32[33,2]{0,1:T(2,128)} %param.20) | copy-start | bytes 796
  7.2 47.8 %all-gather.3.cloned.1.call-start = ((), (), s32[]{:S(2)}) async-start(), calls=%async_computation.2 | async-start | bytes 2228224 | tf_op jit(solution)/shard_map/all_gather | solution.py:59
  8.9 418.3 %reduce-scatter.3.cloned.1.call-start = ((), (), s32[]{:S(2)}) async-start(), calls=%async_computation.3 | async-start | bytes 2228224 | tf_op jit(solution)/shard_map/reduce_scatter | solution.py:61
  366.4 1.3 copy-start.1
  366.4 60.8 %copy-start.2 = (f32[32,1024]{1,0:T(8,128)S(1)}, f32[32,1024]{1,0:T(8,128)}, u32[]{:S(2)}) copy-start(f32[32,1024]{1,0:T(8,128)} %param.18) | copy-start | bytes 393220
  366.4 60.8 %copy-start.3 = (f32[32,1024]{1,0:T(8,128)S(1)}, f32[32,1024]{1,0:T(8,128)}, u32[]{:S(2)}) copy-start(f32[32,1024]{1,0:T(8,128)} %param.17) | copy-start | bytes 393220
  366.4 60.8 %copy-start.4 = (s32[32,1024]{1,0:T(8,128)S(1)}, s32[32,1024]{1,0:T(8,128)}, u32[]{:S(2)}) copy-start(s32[32,1024]{1,0:T(8,128)} %param.19) | copy-start | bytes 393220
  367.7 102.7 %all-gather.5.cloned.1.call-start = ((), (), s32[]{:S(2)}) async-start(), calls=%async_computation.4 | async-start | bytes 2228224 | tf_op jit(solution)/shard_map/all_gather | solution.py:59
  428.8 405.5 %reduce-scatter.5.cloned.1.call-start = ((), (), s32[]{:S(2)}) async-start(), calls=%async_computation.5 | async-start | bytes 2228224 | tf_op jit(solution)/shard_map/reduce_scatter | solution.py:61
  773.5 1.3 copy-start
  773.5 60.8 %copy-start.5 = (f32[32,1024]{1,0:T(8,128)S(1)}, f32[32,1024]{1,0:T(8,128)}, u32[]{:S(2)}) copy-start(f32[32,1024]{1,0:T(8,128)} %reduce-scatter.3.cloned.1.call-done) | copy-start | bytes 393220
Sparse Core Ops, SparseCore 0:
  10.7 44.1 all-gather.2
  367.8 59.2 reduce-scatter.2
  429.9 40.4 all-gather.4
  775.0 59.2 reduce-scatter.4
where the time goes:
time: 855 us; the launch traced here: 843 us
  loops' own time  254 us (30%)
  matrix products  235 us (27%)
  waiting for transfers between devices  207 us (24%)
  local copies, waits for them, and re-layouts  128 us (15%)
  between operations  13.9 us (2%)
    dot_general x132, matrix products, apply_term(): lax.dot_general(block, tile, (((1,), (tile_dim,)), ((), ())), precision=l...  235 us
    another operation x2, loops' own time, tile_terms(): return lax.fori_loop(0, tile_plan.shape[0], one_slot, carry)  168 us
    reduce_scatter x2, waiting for transfers between devices, body(): lax.psum_scatter(partial_grad, 'col', scatter_dimension=1, tiled=True)  119 us
    all_gather x2, waiting for transfers between devices, body(): whole = lax.all_gather(error, 'col', axis=1, tiled=True)  87.6 us
    another operation x132, loops' own time, add_term(): return lax.cond(valid, apply_term, keep_total, acc)  85.9 us
    squeeze x66, local copies, waits for them, and re-layouts, one_slot(): tile = hess_tiles[slot]  85.8 us
    dynamic_slice x66, local copies, waits for them, and re-layouts, one_slot(): col_block = tile_plan[slot, 1]  39.7 us
  transfers between devices with their start and end apart: 4, of which 4 were waited for; matrix products, arithmetic and copies ran while one was open for 0% of the time, Pallas kernels for 0%

commit v1 on v0

v1 whole, which is shorter than its diff:
```python
import functools

import jax
import jax.numpy as jnp
from jax import lax
from jax.experimental import pallas as pl
from jax.experimental.pallas import tpu as pltpu
from jax.sharding import PartitionSpec as P

step_size = 0.15
momentum = 0.6
CHUNKS = 2
MESH = pl.DeviceIdType.MESH


def split(value):
    high = value.astype(jnp.bfloat16)
    return high, (value - high.astype(jnp.float32)).astype(jnp.bfloat16)


def product_kernel(plan_ref, error_ref, tiles_ref, grad_ref, pieces_ref):
    rows = error_ref.shape[1]
    group = tiles_ref.shape[0]

    @pl.when(pl.program_id(0) == 0)
    def _():
        grad_ref[...] = jnp.zeros_like(grad_ref)

        @pl.loop(0, error_ref.shape[0])
        def _(block):
            high, low = split(error_ref[block])
            pieces_ref[block, :rows, :] = high
            pieces_ref[block, rows:, :] = low

    for member in range(group):
        slot = pl.program_id(0) * group + member
        a = plan_ref[slot, 0]
        b = plan_ref[slot, 1]
        high, low = split(tiles_ref[member])

        def terms(block, tile_dim):
            dims = (((1,), (tile_dim,)), ((), ()))
            both = lax.dot_general(pieces_ref[block], high, dims, preferred_element_type=jnp.float32)
            rest = lax.dot_general(pieces_ref[block, :rows, :], low, dims, preferred_element_type=jnp.float32)
            return both[:rows] + both[rows:] + rest

        lower = terms(a, 0)
        upper = terms(b, 1)
        grad_ref[b] += lower
        grad_ref[a] += (a != b).astype(jnp.float32) * upper


def products(tile_plan, error, hess_tiles):
    slots, order, _ = hess_tiles.shape
    blocks, rows, _ = error.shape
    group = max(d for d in (1, 2, 3, 4) if slots % d == 0)
    return pl.pallas_call(
        product_kernel,
        out_shape=jax.ShapeDtypeStruct(error.shape, jnp.float32),
        grid_spec=pltpu.PrefetchScalarGridSpec(
            num_scalar_prefetch=1,
            grid=(slots // group,),
            in_specs=[
                pl.BlockSpec(memory_space=pltpu.VMEM),
                pl.BlockSpec((group, order, order), lambda i, plan: (i, 0, 0)),
            ],
            out_specs=pl.BlockSpec(memory_space=pltpu.VMEM),
            scratch_shapes=[pltpu.VMEM((blocks, 2 * rows, order), jnp.bfloat16)],
        ),
        compiler_params=pltpu.CompilerParams(dimension_semantics=("arbitrary",)),
        name="products",
    )(tile_plan, error, hess_tiles)


class Ring:
    def __init__(self, chips, sides):
        self.chips = chips
        self.sides = sides
        self.half = chips // 2
        index = lax.axis_index("col")
        self.me = index
        self.core = index % 2
        self.pos = self.place(index // 2)

    def place(self, chip):
        if self.sides == 1:
            return chip
        length = self.chips // 2
        side, depth = chip % 2, chip // 2
        return (1 - side) * depth + side * (self.chips - 1 - depth)

    def device(self, offset, core):
        pos = (self.pos + offset + self.chips) % self.chips
        if self.sides == 1:
            return pos * 2 + core
        length = self.chips // 2
        side = pos // length
        depth = (1 - side) * pos + side * (self.chips - 1 - pos)
        return (depth * 2 + side) * 2 + core

    def carries(self, distance, way, chunk):
        if 2 * distance < self.chips:
            return True
        return (chunk < CHUNKS // 2) == (way == 0)


def greet(ring):
    barrier = pltpu.get_barrier_semaphore()
    others = (ring.device(1, ring.core), ring.device(-1, ring.core), ring.device(0, 1 - ring.core))
    for other in others:
        pl.semaphore_signal(barrier, inc=1, device_id={"col": other}, device_id_type=MESH)
    pl.semaphore_wait(barrier, 3)


def remote(src, dst, send_sem, recv_sem, device):
    return pltpu.make_async_remote_copy(
        src_ref=src, dst_ref=dst, send_sem=send_sem, recv_sem=recv_sem,
        device_id={"col": device}, device_id_type=MESH,
    )


def gather(ring, whole_ref, ring_send, ring_recv, pair_send, pair_recv):
    rows = whole_ref.shape[2] // CHUNKS
    partner = ring.device(0, 1 - ring.core)
    copies = {}
    started = []

    def pair(offset, key, source, chunk):
        where = whole_ref.at[source, :, pl.ds(chunk * rows, rows), :]
        copy = remote(where, where, pair_send.at[key], pair_recv.at[key], partner)
        copy.start()
        started.append(copy)

    slot = 0
    for step in range(ring.half + 1):
        for chunk in range(CHUNKS):
            for way, sign in ((0, 1), (1, -1)):
                source = ring.device(-sign * step, ring.core)
                if step > 0:
                    if not ring.carries(step, way, chunk):
                        continue
                    copies[way, step - 1, chunk].wait_recv()
                if step < ring.half and ring.carries(step + 1, way, chunk):
                    where = whole_ref.at[source, :, pl.ds(chunk * rows, rows), :]
                    copy = remote(
                        where, where, ring_send.at[way, step, chunk], ring_recv.at[way, step, chunk],
                        ring.device(sign, ring.core),
                    )
                    copy.start()
                    copies[way, step, chunk] = copy
                if step > 0 or way == 0:
                    pair(step, slot, source, chunk)
                    slot += 1
    for copy in started:
        copy.wait()
    for copy in copies.values():
        copy.wait_send()


def scatter(ring, part_ref, mate_ref, out_ref, in_ref, ring_send, ring_recv, pair_send, pair_recv):
    rows = part_ref.shape[2] // CHUNKS
    partner = ring.device(0, 1 - ring.core)
    mates = {}
    order = [ring.half]
    for distance in range(ring.half - 1, 0, -1):
        order += [distance, -distance]
    order.append(0)
    for offset in order:
        key = offset % ring.chips
        copy = remote(
            part_ref.at[ring.device(offset, 1 - ring.core)], mate_ref.at[key],
            pair_send.at[key], pair_recv.at[key], partner,
        )
        copy.start()
        mates[key] = copy
    landed = set()
    copies = {}

    def chip_sum(offset, at):
        key = offset % ring.chips
        if key not in landed:
            mates[key].wait_recv()
            landed.add(key)
        return part_ref[ring.device(offset, ring.core), :, at, :] + mate_ref[key, :, at, :]

    for step in range(ring.half):
        distance = ring.half - step
        for chunk in range(CHUNKS):
            at = slice(chunk * rows, (chunk + 1) * rows)
            for way, sign in ((0, 1), (1, -1)):
                if not ring.carries(distance, way, chunk):
                    continue
                total = chip_sum(sign * distance, at)
                if (way, step - 1, chunk) in copies:
                    copies[way, step - 1, chunk].wait_recv()
                    total = total + in_ref[way, step - 1, :, at, :]
                out_ref[way, step, :, at, :] = total
                copy = remote(
                    out_ref.at[way, step, :, at, :], in_ref.at[way, step, :, at, :],
                    ring_send.at[way, step, chunk], ring_recv.at[way, step, chunk],
                    ring.device(sign, ring.core),
                )
                copy.start()
                copies[way, step, chunk] = copy
    sums = []
    last = ring.half - 1
    for chunk in range(CHUNKS):
        at = slice(chunk * rows, (chunk + 1) * rows)
        total = chip_sum(0, at)
        for way in (0, 1):
            if (way, last, chunk) in copies:
                copies[way, last, chunk].wait_recv()
                total = total + in_ref[way, last, :, at, :]
        sums.append((at, total))
    for copy in mates.values():
        copy.wait_send()
    for copy in copies.values():
        copy.wait_send()
    return sums


def first_kernel(chips, sides, dense_ref, start_ref, whole_ref, *sems):
    ring = Ring(chips, sides)
    subs, width = whole_ref.shape[1], whole_ref.shape[3]
    for sub in range(subs):
        at = slice(sub * width, (sub + 1) * width)
        whole_ref[ring.me, sub] = start_ref[:, at] - dense_ref[:, at]
    greet(ring)
    gather(ring, whole_ref, *sems)


def update(ring, sums, weights_ref, keep_ref, velocity_ref, weights_out, velocity_out, width, subs):
    for at, total in sums:
        for sub in range(subs):
            cols = slice(sub * width, (sub + 1) * width)
            velocity = total[sub]
            if velocity_ref is not None:
                velocity = momentum * velocity_ref[at, cols] + velocity
            velocity_out[at, cols] = velocity
            keep = keep_ref[at, cols].astype(jnp.float32)
            weights_out[at, cols] = keep * (weights_ref[at, cols] - step_size * velocity)


def middle_kernel(
    chips, sides, part_ref, dense_ref, weights_ref, keep_ref, weights_out, velocity_out, whole_ref,
    mate_ref, out_ref, in_ref, rs_send, rs_recv, rp_send, rp_recv, *sems,
):
    ring = Ring(chips, sides)
    subs, width = whole_ref.shape[1], whole_ref.shape[3]
    greet(ring)
    sums = scatter(ring, part_ref, mate_ref, out_ref, in_ref, rs_send, rs_recv, rp_send, rp_recv)
    update(ring, sums, weights_ref, keep_ref, None, weights_out, velocity_out, width, subs)
    for sub in range(subs):
        at = slice(sub * width, (sub + 1) * width)
        whole_ref[ring.me, sub] = weights_out[:, at] - dense_ref[:, at]
    gather(ring, whole_ref, *sems)


def last_kernel(
    chips, sides, part_ref, weights_ref, keep_ref, velocity_ref, weights_out, velocity_out,
    mate_ref, out_ref, in_ref, rs_send, rs_recv, rp_send, rp_recv,
):
    ring = Ring(chips, sides)
    subs, width = part_ref.shape[1], part_ref.shape[3]
    greet(ring)
    sums = scatter(ring, part_ref, mate_ref, out_ref, in_ref, rs_send, rs_recv, rp_send, rp_recv)
    update(ring, sums, weights_ref, keep_ref, velocity_ref, weights_out, velocity_out, width, subs)


def body(sides, dense_weight, start_weight, keep_mask, tile_plan, hess_tiles):
    devices = lax.axis_size("col")
    chips = devices // 2
    half = chips // 2
    rows, span = dense_weight.shape
    order = hess_tiles.shape[1]
    width = min(span, order)
    subs = span // width
    whole = (devices, subs, rows, width)
    vmem = pl.BlockSpec(memory_space=pltpu.VMEM)
    dma = pltpu.SemaphoreType.DMA
    pairs = chips * CHUNKS
    gather_sems = [dma((2, half, CHUNKS))] * 2 + [dma((pairs,))] * 2
    scatter_scratch = [
        pltpu.VMEM((chips, subs, rows, width), jnp.float32),
        pltpu.VMEM((2, half, subs, rows, width), jnp.float32),
        pltpu.VMEM((2, half, subs, rows, width), jnp.float32),
    ] + [dma((2, half, CHUNKS))] * 2 + [dma((chips,))] * 2
    local = jax.ShapeDtypeStruct((rows, span), jnp.float32)
    full = jax.ShapeDtypeStruct(whole, jnp.float32)

    def exchange(kernel, identity, inputs, outputs, scratch):
        return pl.pallas_call(
            functools.partial(kernel, chips, sides),
            out_shape=outputs,
            in_specs=[vmem] * len(inputs),
            out_specs=[vmem] * len(outputs),
            scratch_shapes=scratch,
            compiler_params=pltpu.CompilerParams(collective_id=identity, has_side_effects=True),
            name=kernel.__name__,
        )(*inputs)

    per_block = order // width

    def hessian_product(error):
        if per_block == 1:
            blocked = error.reshape(devices * subs, rows, width)
        else:
            blocked = error.reshape(-1, per_block, rows, width).transpose(0, 2, 1, 3).reshape(-1, rows, order)
        grad = products(tile_plan, blocked, hess_tiles)
        if per_block > 1:
            grad = grad.reshape(-1, rows, per_block, width).transpose(0, 2, 1, 3)
        return grad.reshape(whole)

    (error,) = exchange(first_kernel, 0, (dense_weight, start_weight), (full,), gather_sems)
    weights, velocity, error = exchange(
        middle_kernel, 1, (hessian_product(error), dense_weight, start_weight, keep_mask),
        (local, local, full), scatter_scratch + gather_sems,
    )
    weights, velocity = exchange(
        last_kernel, 2, (hessian_product(error), weights, keep_mask, velocity), (local, local), scatter_scratch,
    )
    return weights, velocity


def ring_sides(mesh):
    line = mesh.devices.reshape(-1, mesh.shape["col"])[0]
    try:
        return 2 if len({d.coords[1] for d in line}) == 2 else 1
    except AttributeError:
        return 1


def solution(mesh):
    placed = (
        P("layers", "col"),
        P("layers", "col"),
        P("layers", "col"),
        P(("layers", "col"), None),
        P(("layers", "col"), None, None),
    )
    return jax.shard_map(
        functools.partial(body, ring_sides(mesh)),
        mesh=mesh,
        in_specs=placed,
        out_specs=(P("layers", "col"), P("layers", "col")),
        check_vma=False,
    )
```

time: 855 us -> 139 us (0.16); the launches traced: 843 us -> 138 us
  loops' own time: 254 us -> 0 us
  matrix products: 235 us -> 0 us
  waiting for transfers between devices: 207 us -> 0 us
  Pallas kernels: 0 us -> 132 us
  local copies, waits for them, and re-layouts: 128 us -> 4.51 us
  between operations: 13.9 us -> 0.66 us
    another operation x134 -> x0, loops' own time: 254 us -> none  [the longest x2 168 us: tile_terms(): return lax.fori_loop(0, tile_plan.shape[0], one_slot, carry)]
    dot_general x132 -> x0, matrix products: 235 us -> none  [apply_term(): lax.dot_general(block, tile, (((1,), (tile_dim,)), ((), ())), precision=l...]
    pallas_call x0 -> x5, Pallas kernels: none -> 132 us  [the longest x3 83.1 us: exchange(): pl.pallas_call(functools.partial(kernel, chips, sides), out_shape=outputs...]
    reduce_scatter x2 -> x0, waiting for transfers between devices: 119 us -> none  [body(): lax.psum_scatter(partial_grad, 'col', scatter_dimension=1, tiled=True)]
    all_gather x2 -> x0, waiting for transfers between devices: 87.6 us -> none  [body(): whole = lax.all_gather(error, 'col', axis=1, tiled=True)]
    squeeze x66 -> x0, local copies, waits for them, and re-layouts: 85.8 us -> none  [one_slot(): tile = hess_tiles[slot]]
    dynamic_slice x66 -> x0, local copies, waits for them, and re-layouts: 39.7 us -> none  [one_slot(): col_block = tile_plan[slot, 1]]
  transfers between devices with their start and end apart: 4 -> 0, of which waited for: 4 -> 0; matrix products, arithmetic and copies ran while one was open for 0% -> 0% of each run, Pallas kernels for 0% -> 0%
where the time goes in v1:
time: 139 us; the launch traced here: 138 us
  Pallas kernels  132 us (95%)
  local copies, waits for them, and re-layouts  4.51 us (3%)
    pallas_call x3, Pallas kernels, exchange(): pl.pallas_call(functools.partial(kernel, chips, sides), out_shape=outputs...  83.1 us
    pallas_call x2, Pallas kernels, products(): pl.pallas_call(product_kernel, out_shape=jax.ShapeDtypeStruct(error.shape...  49.4 us
    unnamed x3, local copies, waits for them, and re-layouts  4.51 us

profile of v1, /device:TPU:0, one launch (start us, length us, event | category | flops | bytes accessed | tf_op | source)
XLA Modules:
  0.0 137.6 jit_solution(11914595457711212984)
XLA Ops:
  0.6 1.4 copy.8.plan_ref
  2.0 24.0 %first_kernel.1 = f32[16,2,32,512]{3,2,1,0:T(8,128)} custom-call(f32[32,1024]{1,0:T(8,128)} %dense_ref.3, f32[32,1024]{1,0:T(8,128)} %weights_ref.1), custom_call_target="tpu_custom_call" | custom-call | tf_op jit(solution)/shard_map/first_kernel/pallas_call | solution.py:292
  26.0 24.7 %products.2 = f32[32,32,512]{2,1,0:T(8,128)} custom-call(s32[33,2]{1,0:T(8,128)} %copy.8.plan_ref, f32[32,32,512]{2,1,0:T(8,128)} %bitcast.6, f32[33,512,512]{2,1,0:T(8,128)} %tiles_ref.3), custom_call_target="tpu_custom_call" | custom-call | tf_op jit(solution)/shard_map/products/pallas_call | solution.py:57
  50.7 38.9 %middle_kernel.1 = (f32[32,1024]{1,0:T(8,128)}, f32[32,1024]{1,0:T(8,128)}, f32[16,2,32,512]{3,2,1,0:T(8,128)}) custom-call(f32[16,2,32,512]{3,2,1,0:T(8,128)} %bitcast.5, f32[32,1024]{1,0:T(8,128)} %dense_ref.3, f32[32,1024]{1,0:T(8,128)} %weights_ref.1, s32[32,1024]{1,0:T(8,128)} %keep_ref.3), custom_call_target="tpu_custom_call" | custom-call | tf_op jit(solution)/shard_map/middle_kernel/pallas_call | solution.py:292
  89.7 24.7 %products.3 = f32[32,32,512]{2,1,0:T(8,128)} custom-call(s32[33,2]{1,0:T(8,128)} %copy.8.plan_ref, f32[32,32,512]{2,1,0:T(8,128)} %bitcast.7, f32[33,512,512]{2,1,0:T(8,128)} %tiles_ref.3), custom_call_target="tpu_custom_call" | custom-call | tf_op jit(solution)/shard_map/products/pallas_call | solution.py:57
  114.4 20.1 %last_kernel.1 = (f32[32,1024]{1,0:T(8,128)}, f32[32,1024]{1,0:T(8,128)}) custom-call(f32[16,2,32,512]{3,2,1,0:T(8,128)} %bitcast.4, f32[32,1024]{1,0:T(8,128)} %get-tuple-element.6.weights_ref, s32[32,1024]{1,0:T(8,128)} %keep_ref.3, f32[32,1024]{1,0:T(8,128)} %get-tuple-element.7.velocity_ref), custom_call_target="tpu_custom_call" | custom-call | tf_op jit(solution)/shard_map/last_kernel/pallas_call | solution.py:292
  134.5 1.6 %copy.11 = f32[32,1024]{1,0:T(8,128)} copy(f32[32,1024]{1,0:T(8,128)} %get-tuple-element.10) | data formatting | bytes 262144
  136.0 1.6 %copy.12 = f32[32,1024]{1,0:T(8,128)} copy(f32[32,1024]{1,0:T(8,128)} %get-tuple-element.11) | data formatting | bytes 262144

commit v2 on v1

--- a/solution.py
+++ b/solution.py
@@ -9,7 +9,7 @@
 
 step_size = 0.15
 momentum = 0.6
-CHUNKS = 2
+CHUNKS = 4
 MESH = pl.DeviceIdType.MESH
 
 
@@ -229,16 +229,13 @@
     gather(ring, whole_ref, *sems)
 
 
-def update(ring, sums, weights_ref, keep_ref, velocity_ref, weights_out, velocity_out, width, subs):
+def update(sums, weights_ref, keep_ref, weights_out, velocity_out, width, subs):
     for at, total in sums:
         for sub in range(subs):
             cols = slice(sub * width, (sub + 1) * width)
-            velocity = total[sub]
-            if velocity_ref is not None:
-                velocity = momentum * velocity_ref[at, cols] + velocity
-            velocity_out[at, cols] = velocity
+            velocity_out[at, cols] = total[sub]
             keep = keep_ref[at, cols].astype(jnp.float32)
-            weights_out[at, cols] = keep * (weights_ref[at, cols] - step_size * velocity)
+            weights_out[at, cols] = keep * (weights_ref[at, cols] - step_size * total[sub])
 
 
 def middle_kernel(
@@ -249,7 +246,7 @@
     subs, width = whole_ref.shape[1], whole_ref.shape[3]
     greet(ring)
     sums = scatter(ring, part_ref, mate_ref, out_ref, in_ref, rs_send, rs_recv, rp_send, rp_recv)
-    update(ring, sums, weights_ref, keep_ref, None, weights_out, velocity_out, width, subs)
+    update(sums, weights_ref, keep_ref, weights_out, velocity_out, width, subs)
     for sub in range(subs):
         at = slice(sub * width, (sub + 1) * width)
         whole_ref[ring.me, sub] = weights_out[:, at] - dense_ref[:, at]
@@ -257,14 +254,14 @@
 
 
 def last_kernel(
-    chips, sides, part_ref, weights_ref, keep_ref, velocity_ref, weights_out, velocity_out,
-    mate_ref, out_ref, in_ref, rs_send, rs_recv, rp_send, rp_recv,
+    chips, sides, part_ref, gradient_out, mate_ref, out_ref, in_ref, rs_send, rs_recv, rp_send, rp_recv,
 ):
     ring = Ring(chips, sides)
     subs, width = part_ref.shape[1], part_ref.shape[3]
     greet(ring)
-    sums = scatter(ring, part_ref, mate_ref, out_ref, in_ref, rs_send, rs_recv, rp_send, rp_recv)
-    update(ring, sums, weights_ref, keep_ref, velocity_ref, weights_out, velocity_out, width, subs)
+    for at, total in scatter(ring, part_ref, mate_ref, out_ref, in_ref, rs_send, rs_recv, rp_send, rp_recv):
+        for sub in range(subs):
+            gradient_out[at, sub * width : (sub + 1) * width] = total[sub]
 
 
 def body(sides, dense_weight, start_weight, keep_mask, tile_plan, hess_tiles):
@@ -316,9 +313,9 @@
         middle_kernel, 1, (hessian_product(error), dense_weight, start_weight, keep_mask),
         (local, local, full), scatter_scratch + gather_sems,
     )
-    weights, velocity = exchange(
-        last_kernel, 2, (hessian_product(error), weights, keep_mask, velocity), (local, local), scatter_scratch,
-    )
+    (gradient,) = exchange(last_kernel, 2, (hessian_product(error),), (local,), scatter_scratch)
+    velocity = momentum * velocity + gradient
+    weights = keep_mask.astype(jnp.float32) * (weights - step_size * velocity)
     return weights, velocity
 
 

time: 139 us -> 134 us (0.964)
  local copies, waits for them, and re-layouts: 4.51 us -> 1.38 us
  Pallas kernels: 132 us -> 130 us
  other arithmetic: 0 us -> 1.64 us
    unnamed x3 -> x7, local copies, waits for them, and re-layouts: 4.51 us -> 1.38 us
    pallas_call x3, Pallas kernels: 83.1 us -> 80.2 us  [exchange(): pl.pallas_call(functools.partial(kernel, chips, sides), out_shape=outputs...]
    mul x0 -> x1, other arithmetic: none -> 1.64 us  [body(): weights = keep_mask.astype(jnp.float32) * (weights - step_size * velocity)]
where the time goes in v2:
time: 134 us; the launch traced here: 133 us
  Pallas kernels  130 us (97%)
  other arithmetic  1.64 us (1%)
  local copies, waits for them, and re-layouts  1.38 us (1%)
    pallas_call x3, Pallas kernels, exchange(): pl.pallas_call(functools.partial(kernel, chips, sides), out_shape=outputs...  80.2 us
    pallas_call x2, Pallas kernels, products(): pl.pallas_call(product_kernel, out_shape=jax.ShapeDtypeStruct(error.shape...  49.4 us

profile of v2, /device:TPU:0, one launch (start us, length us, event | category | flops | bytes accessed | tf_op | source)
XLA Modules:
  0.0 133.2 jit_solution(18104354889118506937)
XLA Ops:
  0.6 1.4 %copy.7.plan_ref = s32[33,2]{1,0:T(8,128)} copy(s32[33,2]{0,1:T(2,128)} %param.8) | data formatting | bytes 528 | tf_op args[3]
  2.0 23.2 %first_kernel.1 = f32[16,2,32,512]{3,2,1,0:T(8,128)} custom-call(f32[32,1024]{1,0:T(8,128)} %dense_ref.3, f32[32,1024]{1,0:T(8,128)} %weights_ref.1), custom_call_target="tpu_custom_call" | custom-call | tf_op jit(solution)/shard_map/first_kernel/pallas_call | solution.py:289
  25.2 24.7 %products.2 = f32[32,32,512]{2,1,0:T(8,128)} custom-call(s32[33,2]{1,0:T(8,128)} %copy.7.plan_ref, f32[32,32,512]{2,1,0:T(8,128)} %bitcast.6, f32[33,512,512]{2,1,0:T(8,128)} %tiles_ref.3), custom_call_target="tpu_custom_call" | custom-call | tf_op jit(solution)/shard_map/products/pallas_call | solution.py:57
  49.9 37.5 %middle_kernel.1 = (f32[32,1024]{1,0:T(8,128)}, f32[32,1024]{1,0:T(8,128)}, f32[16,2,32,512]{3,2,1,0:T(8,128)}) custom-call(f32[16,2,32,512]{3,2,1,0:T(8,128)} %bitcast.4, f32[32,1024]{1,0:T(8,128)} %dense_ref.3, f32[32,1024]{1,0:T(8,128)} %weights_ref.1, s32[32,1024]{1,0:T(8,128)} %keep_ref.1), custom_call_target="tpu_custom_call" | custom-call | tf_op jit(solution)/shard_map/middle_kernel/pallas_call | solution.py:289
  87.4 24.7 %products.3 = f32[32,32,512]{2,1,0:T(8,128)} custom-call(s32[33,2]{1,0:T(8,128)} %copy.7.plan_ref, f32[32,32,512]{2,1,0:T(8,128)} %bitcast.7, f32[33,512,512]{2,1,0:T(8,128)} %tiles_ref.3), custom_call_target="tpu_custom_call" | custom-call | tf_op jit(solution)/shard_map/products/pallas_call | solution.py:57
  112.0 0.0 copy-start
  112.0 0.0 copy-start.1
  112.0 0.0 copy-start.2
  112.0 19.5 %last_kernel.1 = f32[32,1024]{1,0:T(8,128)} custom-call(f32[16,2,32,512]{3,2,1,0:T(8,128)} %bitcast.5), custom_call_target="tpu_custom_call" | custom-call | tf_op jit(solution)/shard_map/last_kernel/pallas_call | solution.py:289
  131.6 0.0 copy-done
  131.6 0.0 copy-done.1
  131.6 0.0 copy-done.2
  131.6 1.6 %subtract_multiply_fusion = (f32[32,1024]{1,0:T(8,128)}, f32[32,1024]{1,0:T(8,128)}) fusion(f32[32,1024]{1,0:T(8,128)S(1)} %copy-done.1, s32[32,1024]{1,0:T(8,128)S(1)} %copy-done, f32[32,1024]{1,0:T(8,128)} %last_kernel.1, f32[32,1024]{1,0:T(8,128)S(1)} %copy-done.2), kind=kLoop, calls=%fused_computation | loop fusion | flops 196608 | bytes 786432 | tf_op jit(solution)/shard_map/mul | solution.py:318
Async XLA Ops:
  112.0 19.5 %copy-start = (s32[32,1024]{1,0:T(8,128)S(1)}, s32[32,1024]{1,0:T(8,128)}, u32[]{:S(2)}) copy-start(s32[32,1024]{1,0:T(8,128)} %keep_ref.1) | copy-start | bytes 393220
  112.0 19.5 %copy-start.1 = (f32[32,1024]{1,0:T(8,128)S(1)}, f32[32,1024]{1,0:T(8,128)}, u32[]{:S(2)}) copy-start(f32[32,1024]{1,0:T(8,128)} %get-tuple-element.5) | copy-start | bytes 393220
  112.0 19.6 %copy-start.2 = (f32[32,1024]{1,0:T(8,128)S(1)}, f32[32,1024]{1,0:T(8,128)}, u32[]{:S(2)}) copy-start(f32[32,1024]{1,0:T(8,128)} %get-tuple-element.6) | copy-start | bytes 393220
